TPU v7x, 32 devices: a whole 2x2x4 slice. The times are simulated.
32 devices in a mesh: obs: 4 (over x, core), ord: 8 (over z, y).
Axes of the slice: x: 2, y: 2, z: 4, core: 2. Of those that a mesh axis runs over, the one named last changes fastest.
Arguments:
- longitude: float32 [4, 32768], P('obs'), may hold values from -3.140625 to 3.140625
- cycle_of: int32 [4, 32768], P('obs'), may hold values from 0 to 255, never falling along the last dimension, each value on 1 to 256 neighbouring positions
- obs_count: int32 [4], P('obs'), may hold values from 16384 to 32768
- observed: float32 [4, 32768], P('obs'), may hold values from -896 to 896
- obs_weight: float32 [4, 32768], P('obs'), may hold values from 0.3 to 3
- legendre: float32 [4, 72, 288, 256], P('obs', 'ord'), as said below
- precond_inv: float32 [72, 288, 288], P('ord'), as said below
- order_of_slot: int32 [72], P('ord'), may hold values from 0 to 71, each once
Outputs:
- solution: float32 [72, 2, 288], P('ord')
- residual: float32 [72, 2, 288], P('ord')
Inputs may be any that keep to these rules, and one draw needn't show every extreme that they name: `cycle_of`: cycle numbers never fall along a slab; each cycle holds at least one observation slot. `obs_count`: observation slots at or beyond a slab's count carry no weight. legendre[b, m, n, j] is the fully normalized associated Legendre function of degree n and order m at the colatitude of cycle j of slab b, and 0 for n < m. `precond_inv`: every block is symmetric positive definite. order_of_slot names each order once; slot s lies on ord index s // 9.
All inputs are finite; a program needn't handle non-finite values.
Results may differ from a plain program's by a relative error of at most 0.0003.
Values sent between devices are 32-bit elements; how exact they have to be, the bound alone decides.
No kernel may reach another device: no remote copies, remote signals or barrier semaphores. Data moves between devices by JAX's collectives and lax.ppermute only.
A program may use at most 128 MiB of HBM per device.

v0:
```python
import math
import jax
import jax.numpy as jnp
from jax import lax
from jax.sharding import PartitionSpec as P

ITERS = 2
PRECISE = lax.Precision.HIGHEST


def block_split(cycle_ids):
    slab_size = cycle_ids.shape[0]
    block = math.gcd(slab_size, 4096)
    return (block, slab_size // block)


def spread_cycles(cycle_values, cycle_ids):
    rows = cycle_values.shape[0] * cycle_values.shape[1]
    cycle_count = cycle_values.shape[2]
    flat_cycles = cycle_values.reshape(rows, cycle_count)
    block, blocks = block_split(cycle_ids)
    cycle_iota = jnp.arange(cycle_count, dtype=jnp.int32)

    def one_block(id_block):
        onehot = (id_block[:, None] == cycle_iota[None, :]).astype(jnp.float32)
        return jnp.dot(onehot, flat_cycles.T, precision=PRECISE, preferred_element_type=jnp.float32)

    pieces = lax.map(one_block, cycle_ids.reshape(blocks, block))
    at_points = pieces.reshape(blocks * block, rows).T
    return at_points.reshape(cycle_values.shape[0], cycle_values.shape[1], blocks * block)


def collect_cycles(weighted, cycle_ids, cycle_count):
    lead = weighted.shape[0]
    pair = weighted.shape[1]
    rows = lead * pair
    block, blocks = block_split(cycle_ids)
    cycle_iota = jnp.arange(cycle_count, dtype=jnp.int32)
    flat = jnp.moveaxis(weighted.reshape(rows, blocks, block), 1, 0)

    def add_block(total, block_data):
        id_block, value_block = block_data
        onehot = (id_block[:, None] == cycle_iota[None, :]).astype(jnp.float32)
        return (
            total
            + jnp.dot(value_block, onehot, precision=PRECISE, preferred_element_type=jnp.float32),
            None,
        )

    total, unused = lax.scan(
        add_block,
        jnp.zeros((rows, cycle_count), jnp.float32),
        (cycle_ids.reshape(blocks, block), flat),
    )
    return total.reshape(lead, pair, cycle_count)


def synthesize(coefficients, legendre_here, harmonic, cycle_ids):
    cycle_values = jnp.einsum("okn,onr->okr", coefficients, legendre_here, precision=PRECISE)
    at_points = spread_cycles(cycle_values, cycle_ids)
    return jnp.sum(at_points * harmonic, axis=(0, 1))


def adjoint(values, legendre_here, harmonic, cycle_ids):
    weighted = harmonic * values[None, None, :]
    per_cycle = collect_cycles(weighted, cycle_ids, legendre_here.shape[2])
    return jnp.einsum("okr,onr->okn", per_cycle, legendre_here, precision=PRECISE)


def body(
    longitude, cycle_of, obs_count, observed, obs_weight, legendre, precond_inv, order_of_slot
):
    count_here = legendre.shape[1]
    degrees = legendre.shape[2]
    legendre_here = legendre[0]
    east = longitude[0]
    cycle_ids = cycle_of[0]
    slab_size = east.shape[0]
    positions = jnp.arange(slab_size, dtype=jnp.int32)
    total_obs = slab_size * lax.axis_size("obs")
    obs_scale = obs_weight[0] * (positions < obs_count[0]).astype(jnp.float32) / total_obs
    first_order = lax.axis_index("ord") * count_here
    block_orders = first_order + jnp.arange(count_here, dtype=jnp.int32)
    angles = block_orders.astype(jnp.float32)[:, None] * east[None, :]
    harmonic = jnp.stack([jnp.cos(angles), jnp.sin(angles)], axis=1)
    every_owner = lax.all_gather(order_of_slot, "ord", axis=0, tiled=True)
    slot_ids = jnp.arange(every_owner.shape[0], dtype=jnp.int32)
    slot_of_block = jnp.sum(
        jnp.where(every_owner[None, :] == block_orders[:, None], slot_ids[None, :], 0), axis=1
    )
    live_mask = (
        jnp.arange(degrees, dtype=jnp.int32)[None, None, :] >= order_of_slot[:, None, None]
    ).astype(jnp.float32)

    def owner_rows(partial_value):
        summed = lax.psum(partial_value, "obs")
        everyone = lax.all_gather(summed, "ord", axis=0, tiled=True)
        return jnp.take(everyone, order_of_slot, axis=0)

    def precondition(values):
        return live_mask * jnp.einsum("snj,skj->skn", precond_inv, values, precision=PRECISE)

    def energy(values, precond):
        return lax.psum(jnp.sum(values * precond), "ord")

    residual = owner_rows(adjoint(obs_scale * observed[0], legendre_here, harmonic, cycle_ids))
    solution = jnp.zeros_like(residual)
    precond = precondition(residual)
    direction = precond
    energy_now = energy(residual, precond)
    for iteration in range(ITERS):
        block_everyone = lax.all_gather(direction, "ord", axis=0, tiled=True)
        coefficients = jnp.take(block_everyone, slot_of_block, axis=0)
        gradient = lax.psum(synthesize(coefficients, legendre_here, harmonic, cycle_ids), "ord")
        weighted = obs_scale * gradient
        curvature_sum = lax.psum(jnp.sum(weighted * gradient), "obs")
        image = owner_rows(adjoint(weighted, legendre_here, harmonic, cycle_ids))
        image, curvature_sum = (image, curvature_sum)
        step_size = energy_now / curvature_sum
        solution = solution + step_size * direction
        residual = residual - step_size * image
        if iteration + 1 < ITERS:
            precond = precondition(residual)
            energy_next = energy(residual, precond)
            direction = precond + energy_next / energy_now * direction
            energy_now = energy_next
    return (solution, residual)


def solution(mesh):
    placed = (
        P("obs", None),
        P("obs", None),
        P("obs"),
        P("obs", None),
        P("obs", None),
        P("obs", "ord", None, None),
        P("ord", None, None),
        P("ord"),
    )
    return jax.shard_map(
        body,
        mesh=mesh,
        in_specs=placed,
        out_specs=(P("ord", None, None), P("ord", None, None)),
        check_vma=False,
    )
```

profile of v0, /device:TPU:0, one launch (start us, length us, event | category | flops | bytes accessed | tf_op | source)
XLA Modules:
  0.0 720.2 jit_solution(2464493801423855208)
XLA Ops:
  12.2 13.1 %all-reduce = s32[72]{0:T(128)S(1)} all-reduce(s32[72]{0:T(128)S(1)} %dynamic-update-slice), channel_id=1, replica_groups=mesh['obs'=4,'ord'=8] {'ord'}, use_global_device_ids=true, to_apply=%add | all-reduce | flops 72 | bytes 576
  25.5 33.9 %multiply_cosine_fusion = (f32[9,1,32768]{2,1,0:T(1,128)S(1)}, f32[9,1,32768]{2,1,0:T(1,128)S(1)}) fusion(f32[32768]{0:T(1024)} %bitcast.105, f32[9]{0:T(128)S(1)} %fusion.46), kind=kLoop, calls=%fused_computation.58 | loop fusion | flops 294912 | bytes 2490404 | tf_op jit(solution)/shard_map/cos | solution.py:85
  59.4 3.5 pad_maximum_fusion
  62.9 4.2 stack.10
  67.2 4.6 stack.11
  76.1 3.3 multiply_bitcast_fusion.2
  79.4 28.7 %while.57 = (s32[]{:T(128)}, f32[18,256]{1,0:T(8,128)S(1)}, f32[8,18,4096]{2,0,1:T(8,128)}, s32[8,4096]{1,0:T(8,128)S(1)}, s32[]{:T(128)}, /*index=5*/s32[]{:T(128)}) while((s32[]{:T(128)}, f32[18,256]{1,0:T(8,128)S(1)}, f32[8,18,4096]{2,0,1:T(8,128)}, s32[8,4096]{1,0:T(8,128)S(1)}, s32[]{:T(128)}, /*index=5*/s32[]{:T(128)}) %tuple.107), condition=%wide.region_1.2_spmd.clone, body=%wide.region_0.1_spmd.clone.sunk | while | flops 227550208 | bytes 970839 | solution.py:50
  108.1 2.3 fusion.31
  110.4 10.3 %psum.63 = f32[9,2,288]{2,1,0:T(2,128)S(1)} all-reduce(f32[9,2,288]{2,1,0:T(2,128)S(1)} %fusion.31), channel_id=1, replica_groups=mesh['obs'=4,'ord'=8] {'obs'}, use_global_device_ids=true, to_apply=%region_2.3 | all-reduce | flops 5184 | bytes 41472 | tf_op jit(solution)/shard_map/psum | solution.py:96
  120.7 30.7 %all_gather.18 = f32[72,2,288]{2,1,0:T(2,128)S(1)} all-gather(f32[9,2,288]{2,1,0:T(2,128)S(1)} %psum.63), channel_id=1, replica_groups=mesh['obs'=4,'ord'=8] {'ord'}, dimensions={0}, use_global_device_ids=true | all-gather | bytes 186624 | tf_op jit(solution)/shard_map/all_gather | solution.py:97
  152.0 6.2 multiply_reduce_fusion.3
  158.2 30.7 %all_gather.19 = f32[72,2,288]{2,1,0:T(2,128)S(1)} all-gather(f32[9,2,288]{2,1,0:T(2,128)S(1)} %get-tuple-element.301), channel_id=1, replica_groups=mesh['obs'=4,'ord'=8] {'ord'}, dimensions={0}, use_global_device_ids=true | all-gather | bytes 186624 | tf_op jit(solution)/shard_map/all_gather | solution.py:112
  192.6 75.7 %while.55 = (s32[]{:T(128)}, f32[8,4096,18]{1,0,2:T(8,128)}, s32[8,4096]{1,0:T(8,128)S(1)}, f32[18,256]{1,0:T(8,128)S(1)}, s32[]{:T(128)}, /*index=5*/s32[]{:T(128)}) while((s32[]{:T(128)}, f32[8,4096,18]{1,0,2:T(8,128)}, s32[8,4096]{1,0:T(8,128)S(1)}, f32[18,256]{1,0:T(8,128)S(1)}, s32[]{:T(128)}, /*index=5*/s32[]{:T(128)}) %tuple.126), condition=%wide.region_7.9_spmd.clone, body=%wide.region_6.8_spmd.clone.sunk | while | flops 227540992 | bytes 1542221 | solution.py:28
  192.6 2.6 convolution_bitcast_fusion.4
  195.5 6.6 dynamic_update_slice.11
  202.0 2.6 convolution_bitcast_fusion.4
  204.9 6.6 dynamic_update_slice.11
  211.5 2.6 convolution_bitcast_fusion.4
  214.4 6.6 dynamic_update_slice.11
  221.0 2.6 convolution_bitcast_fusion.4
  223.9 6.6 dynamic_update_slice.11
  230.4 2.6 convolution_bitcast_fusion.4
  233.3 6.6 dynamic_update_slice.11
  239.9 2.6 convolution_bitcast_fusion.4
  242.8 6.6 dynamic_update_slice.11
  249.4 2.6 convolution_bitcast_fusion.4
  252.2 6.6 dynamic_update_slice.11
  258.8 2.6 convolution_bitcast_fusion.4
  261.7 6.6 dynamic_update_slice.11
  268.3 2.0 pad.7
  273.5 19.6 %psum.64 = f32[]{:T(128)} all-reduce(f32[]{:T(128)} %get-tuple-element.300), channel_id=1, replica_groups=mesh['obs'=4,'ord'=8] {'ord'}, use_global_device_ids=true, to_apply=%region_4.6 | all-reduce | flops 1 | bytes 8 | tf_op jit(solution)/shard_map/psum | solution.py:104
  293.1 49.5 %all-reduce.6.cloned.1.call-done = f32[32768]{0:T(1024)} async-done(((f32[32768]{0:T(1024)}), f32[32768]{0:T(1024)}) %all-reduce.6.cloned.1.call-update) | async-done | bytes 131088 | tf_op jit(solution)/shard_map/psum | solution.py:114
  344.1 3.3 multiply_bitcast_fusion.1
  347.4 28.2 %while.58 = (s32[]{:T(128)}, f32[18,256]{1,0:T(8,128)S(1)}, f32[8,18,4096]{2,0,1:T(8,128)}, s32[8,4096]{1,0:T(8,128)S(1)}, s32[]{:T(128)}, /*index=5*/s32[]{:T(128)}) while((s32[]{:T(128)}, f32[18,256]{1,0:T(8,128)S(1)}, f32[8,18,4096]{2,0,1:T(8,128)}, s32[8,4096]{1,0:T(8,128)S(1)}, s32[]{:T(128)}, /*index=5*/s32[]{:T(128)}) %tuple.127), condition=%wide.region_13.15_spmd.clone, body=%wide.region_12.14_spmd.clone.sunk | while | flops 227550208 | bytes 970839 | solution.py:50
  375.7 2.3 fusion.27
  377.9 11.3 %all-reduce.2 = (f32[9,2,288]{2,1,0:T(2,128)S(1)}, f32[]{:T(128)}) all-reduce(f32[9,2,288]{2,1,0:T(2,128)S(1)} %fusion.27, f32[]{:T(128)} %get-tuple-element.296), channel_id=1, replica_groups=mesh['obs'=4,'ord'=8] {'obs'}, use_global_device_ids=true, to_apply=%region_14.16 | all-reduce | flops 5185 | bytes 41480 | tf_op jit(solution)/shard_map/psum | solution.py:96
  389.2 30.8 %all_gather.21 = f32[72,2,288]{2,1,0:T(2,128)S(1)} all-gather(f32[9,2,288]{2,1,0:T(2,128)S(1)} %get-tuple-element.292), channel_id=1, replica_groups=mesh['obs'=4,'ord'=8] {'ord'}, dimensions={0}, use_global_device_ids=true | all-gather | bytes 186624 | tf_op jit(solution)/shard_map/all_gather | solution.py:97
  421.9 6.2 multiply_reduce_fusion.2
  428.1 20.1 %psum.68 = f32[]{:T(128)} all-reduce(f32[]{:T(128)} %get-tuple-element.302), channel_id=1, replica_groups=mesh['obs'=4,'ord'=8] {'ord'}, use_global_device_ids=true, to_apply=%region_16.18 | all-reduce | flops 1 | bytes 8 | tf_op jit(solution)/shard_map/psum | solution.py:104
  449.4 30.7 %all_gather.22 = f32[72,2,288]{2,1,0:T(2,128)S(1)} all-gather(f32[9,2,288]{2,1,0:T(2,128)S(1)} %multiply_add_fusion.1), channel_id=1, replica_groups=mesh['obs'=4,'ord'=8] {'ord'}, dimensions={0}, use_global_device_ids=true | all-gather | bytes 186624 | tf_op jit(solution)/shard_map/all_gather | solution.py:112
  483.8 75.9 %while.56 = (s32[]{:T(128)}, f32[8,4096,18]{1,0,2:T(8,128)}, s32[8,4096]{1,0:T(8,128)S(1)}, f32[18,256]{1,0:T(8,128)S(1)}, s32[]{:T(128)}, /*index=5*/s32[]{:T(128)}) while((s32[]{:T(128)}, f32[8,4096,18]{1,0,2:T(8,128)}, s32[8,4096]{1,0:T(8,128)S(1)}, f32[18,256]{1,0:T(8,128)S(1)}, s32[]{:T(128)}, /*index=5*/s32[]{:T(128)}) %tuple.128), condition=%wide.region_18.20_spmd.clone, body=%wide.region_17.19_spmd.clone.sunk | while | flops 227540992 | bytes 1542221 | solution.py:28
  484.1 2.6 convolution_bitcast_fusion.5
  486.9 6.6 dynamic_update_slice.12
  493.5 2.6 convolution_bitcast_fusion.5
  496.4 6.6 dynamic_update_slice.12
  503.0 2.6 convolution_bitcast_fusion.5
  505.9 6.6 dynamic_update_slice.12
  512.5 2.6 convolution_bitcast_fusion.5
  515.3 6.6 dynamic_update_slice.12
  521.9 2.6 convolution_bitcast_fusion.5
  524.8 6.6 dynamic_update_slice.12
  531.4 2.6 convolution_bitcast_fusion.5
  534.3 6.6 dynamic_update_slice.12
  540.8 2.6 convolution_bitcast_fusion.5
  543.7 6.6 dynamic_update_slice.12
  550.3 2.6 convolution_bitcast_fusion.5
  553.2 6.6 dynamic_update_slice.12
  559.8 2.0 pad.8
  564.9 67.5 %all-reduce.8.cloned.1.call-done = f32[32768]{0:T(1024)} async-done(((f32[32768]{0:T(1024)}), f32[32768]{0:T(1024)}) %all-reduce.8.cloned.1.call-update) | async-done | bytes 131088 | tf_op jit(solution)/shard_map/psum | solution.py:114
  634.0 3.3 multiply_bitcast_fusion
  637.4 28.2 %while.59 = (s32[]{:T(128)}, f32[18,256]{1,0:T(8,128)S(1)}, f32[8,18,4096]{2,0,1:T(8,128)}, s32[8,4096]{1,0:T(8,128)S(1)}, s32[]{:T(128)}, /*index=5*/s32[]{:T(128)}) while((s32[]{:T(128)}, f32[18,256]{1,0:T(8,128)S(1)}, f32[8,18,4096]{2,0,1:T(8,128)}, s32[8,4096]{1,0:T(8,128)S(1)}, s32[]{:T(128)}, /*index=5*/s32[]{:T(128)}) %tuple.129), condition=%wide.region_24.26_spmd.clone, body=%wide.region_23.25_spmd.clone.sunk | while | flops 227550208 | bytes 970839 | solution.py:50
  665.6 2.3 fusion.23
  667.9 11.3 %all-reduce.1 = (f32[]{:T(128)}, f32[9,2,288]{2,1,0:T(2,128)S(1)}) all-reduce(f32[]{:T(128)} %get-tuple-element.294, f32[9,2,288]{2,1,0:T(2,128)S(1)} %fusion.23), channel_id=1, replica_groups=mesh['obs'=4,'ord'=8] {'obs'}, use_global_device_ids=true, to_apply=%region_22.24 | all-reduce | flops 5185 | bytes 41480 | tf_op jit(solution)/shard_map/psum | solution.py:116
  679.2 30.8 %all_gather.23 = f32[72,2,288]{2,1,0:T(2,128)S(1)} all-gather(f32[9,2,288]{2,1,0:T(2,128)S(1)} %get-tuple-element.291), channel_id=1, replica_groups=mesh['obs'=4,'ord'=8] {'ord'}, dimensions={0}, use_global_device_ids=true | all-gather | bytes 186624 | tf_op jit(solution)/shard_map/all_gather | solution.py:97
  (171 shorter events, 117.4 us)
Async XLA Ops:
  7.2 101.0 %copy-start = (f32[1,9,288,256]{3,2,1,0:T(8,128)S(1)}, f32[1,9,288,256]{3,2,1,0:T(8,128)}, u32[]{:S(2)}) copy-start(f32[1,9,288,256]{3,2,1,0:T(8,128)} %param.25) | copy-start | bytes 7962628
  7.2 335.4 %all-reduce.6.cloned.1.call-start = ((), (), s32[]{:S(2)}) async-start(), calls=%async_computation | async-start | bytes 262144 | tf_op jit(solution)/shard_map/psum | solution.py:114
  67.2 5.7 copy-start.3
  67.2 6.6 copy-start.4
  67.2 8.0 %copy-start.5 = (s32[1,32768]{1,0:T(1,128)S(1)}, s32[1,32768]{1,0:T(1,128)}, u32[]{:S(2)}) copy-start(s32[1,32768]{1,0:T(1,128)} %param.21) | copy-start | bytes 393220
  270.2 1.9 copy-start.1
  273.5 359.0 %all-reduce.8.cloned.1.call-start = ((), (), s32[]{:S(2)}) async-start(), calls=%async_computation.1 | async-start | bytes 262144 | tf_op jit(solution)/shard_map/psum | solution.py:114
  561.7 1.9 copy-start.2
Sparse Core Ops, SparseCore 0:
  273.6 68.9 all-reduce.5
  565.1 67.3 all-reduce.7
where the time goes:
time: 733 us; the launch traced here: 720 us
  blocking collectives  239 us (33%)
  local copies, waits for them, and re-layouts  183 us (25%)
  waiting for transfers between devices  117 us (16%)
  matrix products  99.8 us (14%)
  other arithmetic  59.5 us (8%)
  between operations  19.7 us (3%)
    psum x2, waiting for transfers between devices, body(): lax.psum(synthesize(coefficients, legendre_here, harmonic, cycle_ids), 'o...  117 us
    dynamic_update_slice x32, local copies, waits for them, and re-layouts, spread_cycles(): pieces = lax.map(one_block, cycle_ids.reshape(blocks, block))  110 us
    all_gather x3, blocking collectives, owner_rows(): everyone = lax.all_gather(summed, 'ord', axis=0, tiled=True)  92.2 us
    all_gather x2, blocking collectives, body(): block_everyone = lax.all_gather(direction, 'ord', axis=0, tiled=True)  61.4 us
    dynamic_slice x64, local copies, waits for them, and re-layouts, collect_cycles(): lax.scan(add_block, jnp.zeros((rows, cycle_count), jnp.float32), (cycle_i...  47 us
    dot_general x16, matrix products, one_block(): jnp.dot(onehot, flat_cycles.T, precision=PRECISE, preferred_element_type=...  40.8 us
    psum x2, blocking collectives, energy(): return lax.psum(jnp.sum(values * precond), 'ord')  39.6 us
    dot_general x24, matrix products, add_block(): jnp.dot(value_block, onehot, precision=PRECISE, preferred_element_type=jn...  36.9 us
  transfers between devices with their start and end apart: 2, of which 2 were waited for; matrix products, arithmetic and copies ran while one was open for 0% of the time, Pallas kernels for 0%

commit v1 on v0

--- a/solution.py
+++ b/solution.py
@@ -111,7 +111,8 @@
     for iteration in range(ITERS):
         block_everyone = lax.all_gather(direction, "ord", axis=0, tiled=True)
         coefficients = jnp.take(block_everyone, slot_of_block, axis=0)
-        gradient = lax.psum(synthesize(coefficients, legendre_here, harmonic, cycle_ids), "ord")
+        inner_x = synthesize(coefficients, legendre_here, harmonic, cycle_ids)
+        gradient = lax.all_gather(inner_x, "ord").sum(axis=0)
         weighted = obs_scale * gradient
         curvature_sum = lax.psum(jnp.sum(weighted * gradient), "obs")
         image = owner_rows(adjoint(weighted, legendre_here, harmonic, cycle_ids))

time: 733 us -> 691 us (0.943)
  waiting for transfers between devices: 117 us -> 56.8 us
  matrix products: 99.8 us -> 110 us
    psum x2 -> x0, waiting for transfers between devices: 117 us -> none  [body(): lax.psum(synthesize(coefficients, legendre_here, harmonic, cycle_ids), 'o...]
    all_gather x0 -> x2, waiting for transfers between devices: none -> 56.8 us  [body(): gradient = lax.all_gather(inner_x, 'ord').sum(axis=0)]
    dot_general x24, matrix products: 36.9 us -> 46.9 us  [add_block(): jnp.dot(value_block, onehot, precision=PRECISE, preferred_element_type=jn...]
where the time goes in v1:
time: 691 us; the launch traced here: 677 us
  blocking collectives  239 us (35%)
  local copies, waits for them, and re-layouts  189 us (27%)
  matrix products  110 us (16%)
  other arithmetic  61.4 us (9%)
  waiting for transfers between devices  56.8 us (8%)
  between operations  20 us (3%)
    dynamic_update_slice x32, local copies, waits for them, and re-layouts, spread_cycles(): pieces = lax.map(one_block, cycle_ids.reshape(blocks, block))  110 us
    all_gather x3, blocking collectives, owner_rows(): everyone = lax.all_gather(summed, 'ord', axis=0, tiled=True)  92 us
    all_gather x2, blocking collectives, body(): block_everyone = lax.all_gather(direction, 'ord', axis=0, tiled=True)  61.5 us
    all_gather x2, waiting for transfers between devices, body(): gradient = lax.all_gather(inner_x, 'ord').sum(axis=0)  56.8 us
    dynamic_slice x64, local copies, waits for them, and re-layouts, collect_cycles(): lax.scan(add_block, jnp.zeros((rows, cycle_count), jnp.float32), (cycle_i...  47 us
    dot_general x24, matrix products, add_block(): jnp.dot(value_block, onehot, precision=PRECISE, preferred_element_type=jn...  46.9 us
    dot_general x16, matrix products, one_block(): jnp.dot(onehot, flat_cycles.T, precision=PRECISE, preferred_element_type=...  40.8 us
    psum x2, blocking collectives, energy(): return lax.psum(jnp.sum(values * precond), 'ord')  39.1 us
  transfers between devices with their start and end apart: 2, of which 2 were waited for; matrix products, arithmetic and copies ran while one was open for 0% of the time, Pallas kernels for 0%

profile of v1, /device:TPU:0, one launch (start us, length us, event | category | flops | bytes accessed | tf_op | source)
XLA Modules:
  0.0 677.5 jit_solution(13195973503372552422)
XLA Ops:
  12.8 13.1 %all-reduce = s32[72]{0:T(128)S(1)} all-reduce(s32[72]{0:T(128)S(1)} %dynamic-update-slice), channel_id=1, replica_groups=mesh['obs'=4,'ord'=8] {'ord'}, use_global_device_ids=true, to_apply=%add | all-reduce | flops 72 | bytes 576
  26.1 33.9 %multiply_cosine_fusion = (f32[9,1,32768]{2,1,0:T(1,128)S(1)}, f32[9,1,32768]{2,1,0:T(1,128)S(1)}) fusion(f32[32768]{0:T(1024)} %bitcast.107, f32[9]{0:T(128)S(1)} %fusion.49), kind=kLoop, calls=%fused_computation.58 | loop fusion | flops 294912 | bytes 2490404 | tf_op jit(solution)/shard_map/cos | solution.py:85
  60.1 3.5 pad_maximum_fusion
  63.5 4.2 stack.10
  67.8 4.6 stack.11
  76.7 3.3 multiply_bitcast_fusion.2
  80.0 28.7 %while.57 = (s32[]{:T(128)}, f32[18,256]{1,0:T(8,128)S(1)}, f32[8,18,4096]{2,0,1:T(8,128)}, s32[8,4096]{1,0:T(8,128)S(1)}, s32[]{:T(128)}, /*index=5*/s32[]{:T(128)}) while((s32[]{:T(128)}, f32[18,256]{1,0:T(8,128)S(1)}, f32[8,18,4096]{2,0,1:T(8,128)}, s32[8,4096]{1,0:T(8,128)S(1)}, s32[]{:T(128)}, /*index=5*/s32[]{:T(128)}) %tuple.105), condition=%wide.region_1.2_spmd.clone, body=%wide.region_0.1_spmd.clone.sunk | while | flops 227550208 | bytes 970839 | solution.py:50
  111.0 10.3 %psum.49 = f32[9,2,288]{2,1,0:T(2,128)S(1)} all-reduce(f32[9,2,288]{2,1,0:T(2,128)S(1)} %fusion.31), channel_id=1, replica_groups=mesh['obs'=4,'ord'=8] {'obs'}, use_global_device_ids=true, to_apply=%region_2.3 | all-reduce | flops 5184 | bytes 41472 | tf_op jit(solution)/shard_map/psum | solution.py:96
  121.3 30.7 %all_gather.30 = f32[72,2,288]{2,1,0:T(2,128)S(1)} all-gather(f32[9,2,288]{2,1,0:T(2,128)S(1)} %psum.49), channel_id=1, replica_groups=mesh['obs'=4,'ord'=8] {'ord'}, dimensions={0}, use_global_device_ids=true | all-gather | bytes 186624 | tf_op jit(solution)/shard_map/all_gather | solution.py:97
  152.6 6.3 multiply_reduce_fusion.1
  158.9 30.7 %all_gather.31 = f32[72,2,288]{2,1,0:T(2,128)S(1)} all-gather(f32[9,2,288]{2,1,0:T(2,128)S(1)} %get-tuple-element.297), channel_id=1, replica_groups=mesh['obs'=4,'ord'=8] {'ord'}, dimensions={0}, use_global_device_ids=true | all-gather | bytes 186624 | tf_op jit(solution)/shard_map/all_gather | solution.py:112
  193.3 75.7 %while.55 = (s32[]{:T(128)}, f32[8,4096,18]{1,0,2:T(8,128)}, s32[8,4096]{1,0:T(8,128)S(1)}, f32[18,256]{1,0:T(8,128)S(1)}, s32[]{:T(128)}, /*index=5*/s32[]{:T(128)}) while((s32[]{:T(128)}, f32[8,4096,18]{1,0,2:T(8,128)}, s32[8,4096]{1,0:T(8,128)S(1)}, f32[18,256]{1,0:T(8,128)S(1)}, s32[]{:T(128)}, /*index=5*/s32[]{:T(128)}) %tuple.124), condition=%wide.region_7.9_spmd.clone, body=%wide.region_6.8_spmd.clone.sunk | while | flops 227540992 | bytes 1542221 | solution.py:28
  193.3 2.6 convolution_bitcast_fusion.4
  196.2 6.6 dynamic_update_slice.11
  202.8 2.6 convolution_bitcast_fusion.4
  205.6 6.6 dynamic_update_slice.11
  212.2 2.6 convolution_bitcast_fusion.4
  215.1 6.6 dynamic_update_slice.11
  221.7 2.6 convolution_bitcast_fusion.4
  224.6 6.6 dynamic_update_slice.11
  231.2 2.6 convolution_bitcast_fusion.4
  234.0 6.6 dynamic_update_slice.11
  240.6 2.6 convolution_bitcast_fusion.4
  243.5 6.6 dynamic_update_slice.11
  250.1 2.6 convolution_bitcast_fusion.4
  253.0 6.6 dynamic_update_slice.11
  259.5 2.6 convolution_bitcast_fusion.4
  262.4 6.6 dynamic_update_slice.11
  274.2 19.3 %psum.50 = f32[]{:T(128)} all-reduce(f32[]{:T(128)} %get-tuple-element.296), channel_id=1, replica_groups=mesh['obs'=4,'ord'=8] {'ord'}, use_global_device_ids=true, to_apply=%region_4.6 | all-reduce | flops 1 | bytes 8 | tf_op jit(solution)/shard_map/psum | solution.py:104
  293.6 19.6 %all-gather.5.cloned.1.call-done = f32[262144]{0:T(1024)} async-done(((f32[32768]{0:T(1024)}), f32[262144]{0:T(1024)}) %all-gather.5.cloned.1.call-update) | async-done | bytes 1048592 | tf_op jit(solution)/shard_map/all_gather | solution.py:115
  317.1 3.3 multiply_bitcast_fusion.1
  320.4 38.1 %while.58 = (s32[]{:T(128)}, f32[18,256]{1,0:T(8,128)}, f32[8,18,4096]{2,0,1:T(8,128)}, s32[8,4096]{1,0:T(8,128)S(1)}, s32[]{:T(128)}, /*index=5*/s32[]{:T(128)}) while((s32[]{:T(128)}, f32[18,256]{1,0:T(8,128)}, f32[8,18,4096]{2,0,1:T(8,128)}, s32[8,4096]{1,0:T(8,128)S(1)}, s32[]{:T(128)}, /*index=5*/s32[]{:T(128)}) %tuple.125), condition=%wide.region_13.15_spmd.clone, body=%wide.region_12.14_spmd.clone.sunk | while | flops 227550208 | bytes 970839 | solution.py:50
  326.5 2.9 fusion.66
  331.4 2.9 fusion.66
  336.2 2.9 fusion.66
  341.1 2.9 fusion.66
  345.9 2.9 fusion.66
  350.8 2.9 fusion.66
  355.6 2.9 fusion.66
  362.2 11.3 %all-reduce.2 = (f32[9,2,288]{2,1,0:T(2,128)S(1)}, f32[]{:T(128)}) all-reduce(f32[9,2,288]{2,1,0:T(2,128)S(1)} %fusion.27, f32[]{:T(128)} %fusion.33), channel_id=1, replica_groups=mesh['obs'=4,'ord'=8] {'obs'}, use_global_device_ids=true, to_apply=%region_14.16 | all-reduce | flops 5185 | bytes 41480 | tf_op jit(solution)/shard_map/psum | solution.py:96
  373.5 30.7 %all_gather.35 = f32[72,2,288]{2,1,0:T(2,128)S(1)} all-gather(f32[9,2,288]{2,1,0:T(2,128)S(1)} %get-tuple-element.292), channel_id=1, replica_groups=mesh['obs'=4,'ord'=8] {'ord'}, dimensions={0}, use_global_device_ids=true | all-gather | bytes 186624 | tf_op jit(solution)/shard_map/all_gather | solution.py:97
  406.2 6.2 multiply_reduce_fusion
  412.4 19.8 %psum.53 = f32[]{:T(128)} all-reduce(f32[]{:T(128)} %get-tuple-element.298), channel_id=1, replica_groups=mesh['obs'=4,'ord'=8] {'ord'}, use_global_device_ids=true, to_apply=%region_16.18 | all-reduce | flops 1 | bytes 8 | tf_op jit(solution)/shard_map/psum | solution.py:104
  433.5 30.8 %all_gather.36 = f32[72,2,288]{2,1,0:T(2,128)S(1)} all-gather(f32[9,2,288]{2,1,0:T(2,128)S(1)} %multiply_add_fusion.1), channel_id=1, replica_groups=mesh['obs'=4,'ord'=8] {'ord'}, dimensions={0}, use_global_device_ids=true | all-gather | bytes 186624 | tf_op jit(solution)/shard_map/all_gather | solution.py:112
  468.0 75.9 %while.56 = (s32[]{:T(128)}, f32[8,4096,18]{1,0,2:T(8,128)}, s32[8,4096]{1,0:T(8,128)S(1)}, f32[18,256]{1,0:T(8,128)S(1)}, s32[]{:T(128)}, /*index=5*/s32[]{:T(128)}) while((s32[]{:T(128)}, f32[8,4096,18]{1,0,2:T(8,128)}, s32[8,4096]{1,0:T(8,128)S(1)}, f32[18,256]{1,0:T(8,128)S(1)}, s32[]{:T(128)}, /*index=5*/s32[]{:T(128)}) %tuple.126), condition=%wide.region_18.20_spmd.clone, body=%wide.region_17.19_spmd.clone.sunk | while | flops 227540992 | bytes 1542221 | solution.py:28
  468.2 2.6 convolution_bitcast_fusion.5
  471.1 6.6 dynamic_update_slice.12
  477.7 2.6 convolution_bitcast_fusion.5
  480.6 6.6 dynamic_update_slice.12
  487.1 2.6 convolution_bitcast_fusion.5
  490.0 6.6 dynamic_update_slice.12
  499.5 6.6 dynamic_update_slice.12
  508.9 6.6 dynamic_update_slice.12
  515.5 2.6 convolution_bitcast_fusion.5
  518.4 6.6 dynamic_update_slice.12
  525.0 2.6 convolution_bitcast_fusion.5
  527.9 6.6 dynamic_update_slice.12
  534.5 2.6 convolution_bitcast_fusion.5
  537.3 6.6 dynamic_update_slice.12
  549.1 37.2 %all-gather.7.cloned.1.call-done = f32[262144]{0:T(1024)} async-done(((f32[32768]{0:T(1024)}), f32[262144]{0:T(1024)}) %all-gather.7.cloned.1.call-update) | async-done | bytes 1048592 | tf_op jit(solution)/shard_map/all_gather | solution.py:115
  590.3 3.3 multiply_bitcast_fusion
  593.6 28.2 %while.59 = (s32[]{:T(128)}, f32[18,256]{1,0:T(8,128)S(1)}, f32[8,18,4096]{2,0,1:T(8,128)}, s32[8,4096]{1,0:T(8,128)S(1)}, s32[]{:T(128)}, /*index=5*/s32[]{:T(128)}) while((s32[]{:T(128)}, f32[18,256]{1,0:T(8,128)S(1)}, f32[8,18,4096]{2,0,1:T(8,128)}, s32[8,4096]{1,0:T(8,128)S(1)}, s32[]{:T(128)}, /*index=5*/s32[]{:T(128)}) %tuple.127), condition=%wide.region_24.26_spmd.clone, body=%wide.region_23.25_spmd.clone.sunk | while | flops 227550208 | bytes 970839 | solution.py:50
  624.9 11.4 %all-reduce.1 = (f32[]{:T(128)}, f32[9,2,288]{2,1,0:T(2,128)S(1)}) all-reduce(f32[]{:T(128)} %fusion.34, f32[9,2,288]{2,1,0:T(2,128)S(1)} %fusion.23), channel_id=1, replica_groups=mesh['obs'=4,'ord'=8] {'obs'}, use_global_device_ids=true, to_apply=%region_22.24 | all-reduce | flops 5185 | bytes 41480 | tf_op jit(solution)/shard_map/psum | solution.py:117
  636.3 30.7 %all_gather.39 = f32[72,2,288]{2,1,0:T(2,128)S(1)} all-gather(f32[9,2,288]{2,1,0:T(2,128)S(1)} %get-tuple-element.291), channel_id=1, replica_groups=mesh['obs'=4,'ord'=8] {'ord'}, dimensions={0}, use_global_device_ids=true | all-gather | bytes 186624 | tf_op jit(solution)/shard_map/all_gather | solution.py:97
  (197 shorter events, 130.7 us)
Async XLA Ops:
  7.2 101.6 %copy-start = (f32[1,9,288,256]{3,2,1,0:T(8,128)S(1)}, f32[1,9,288,256]{3,2,1,0:T(8,128)}, u32[]{:S(2)}) copy-start(f32[1,9,288,256]{3,2,1,0:T(8,128)} %param.25) | copy-start | bytes 7962628
  7.2 306.0 %all-gather.5.cloned.1.call-start = ((), (), s32[]{:S(2)}) async-start(), calls=%async_computation | async-start | bytes 1179648 | tf_op jit(solution)/shard_map/all_gather | solution.py:115
  8.7 143.9 %copy-start.11 = (pred[9]{0:T(512)(128)(4,1)}, pred[9]{0:T(512)(128)(4,1)S(1)}, u32[]{:S(2)}) copy-start(pred[9]{0:T(512)(128)(4,1)S(1)} %compare_and_fusion.1) | copy-start | bytes 31
  26.1 164.0 %copy-start.14 = (pred[9]{0:T(512)(128)(4,1)}, pred[9]{0:T(512)(128)(4,1)S(1)}, u32[]{:S(2)}) copy-start(pred[9]{0:T(512)(128)(4,1)S(1)} %compare_and_fusion) | copy-start | bytes 31
  67.8 5.7 copy-start.3
  67.8 6.6 copy-start.8
  67.8 8.0 %copy-start.9 = (s32[1,32768]{1,0:T(1,128)S(1)}, s32[1,32768]{1,0:T(1,128)}, u32[]{:S(2)}) copy-start(s32[1,32768]{1,0:T(1,128)} %param.21) | copy-start | bytes 393220
  108.7 43.9 %copy-start.6 = (f32[9,288]{1,0:T(8,128)S(1)}, f32[9,288]{1,0:T(8,128)}, u32[]{:S(2)}) copy-start(f32[9,288]{1,0:T(8,128)} %fusion.44) | copy-start | bytes 31108
  152.0 252.2 %copy-start.10 = (s32[1024]{0:T(1024)}, s32[1024]{0:T(1024)S(1)}, u32[]{:S(2)}) copy-start(s32[1024]{0:T(1024)S(1)} %pad_clamp_fusion.1) | copy-start | bytes 12292
  271.0 1.9 copy-start.1
  274.2 312.1 %all-gather.7.cloned.1.call-start = ((), (), s32[]{:S(2)}) async-start(), calls=%async_computation.1 | async-start | bytes 1179648 | tf_op jit(solution)/shard_map/all_gather | solution.py:115
  358.5 47.6 %copy-start.12 = (pred[9]{0:T(512)(128)(4,1)S(1)}, pred[9]{0:T(512)(128)(4,1)}, u32[]{:S(2)}) copy-start(pred[9]{0:T(512)(128)(4,1)} %copy-done.11) | copy-start | bytes 31
  358.5 47.7 %copy-start.7 = (f32[9,288]{1,0:T(8,128)S(1)}, f32[9,288]{1,0:T(8,128)}, u32[]{:S(2)}) copy-start(f32[9,288]{1,0:T(8,128)} %fusion.44) | copy-start | bytes 31108
  361.5 103.3 %copy-start.15 = (pred[9]{0:T(512)(128)(4,1)S(1)}, pred[9]{0:T(512)(128)(4,1)}, u32[]{:S(2)}) copy-start(pred[9]{0:T(512)(128)(4,1)} %copy-done.14) | copy-start | bytes 31
  406.2 60.1 %copy-start.4 = (f32[9,2,288]{2,1,0:T(2,128)}, f32[9,2,288]{2,1,0:T(2,128)S(1)}, u32[]{:S(2)}) copy-start(f32[9,2,288]{2,1,0:T(2,128)S(1)} %fusion.40) | copy-start | bytes 62212
  545.9 1.9 copy-start.2
  621.9 47.8 %copy-start.5 = (f32[9,2,288]{2,1,0:T(2,128)S(1)}, f32[9,2,288]{2,1,0:T(2,128)}, u32[]{:S(2)}) copy-start(f32[9,2,288]{2,1,0:T(2,128)} %copy-done.4) | copy-start | bytes 62212
  621.9 47.8 %copy-start.13 = (pred[9]{0:T(512)(128)(4,1)S(1)}, pred[9]{0:T(512)(128)(4,1)}, u32[]{:S(2)}) copy-start(pred[9]{0:T(512)(128)(4,1)} %copy-done.11) | copy-start | bytes 31
Sparse Core Ops, SparseCore 0:
  274.3 38.8 all-gather.4
  549.2 37.0 all-gather.6
